TPU v7x, 32 devices: a whole 2x2x4 slice. The times are simulated.
32 devices in a mesh: fsdp: 8 (over z, x), seq: 4 (over y, core).
Axes of the slice: x: 2, y: 2, z: 4, core: 2. Of those that a mesh axis runs over, the one named last changes fastest.
Arguments:
- context: bfloat16 [16, 512, 2560], P('fsdp', 'seq'), may hold values from -6 to 6
- residual: bfloat16 [16, 512, 2560], P('fsdp', 'seq'), may hold values from -6 to 6
- target_rows: bfloat16 [16, 512, 2560], P('fsdp', 'seq'), may hold values from -0.00390625 to 0.00390625
- log_norm: float32 [16, 512], P('fsdp', 'seq'), may hold values from -0.15 to 0.15
- norm_gain: float32 [2560], replicated, may hold values from 0.1 to 1.9
- out_proj: bfloat16 [2560, 2560], P('fsdp'), may hold values from -0.125 to 0.125
- old_logprob: float32 [16, 512], P('fsdp', 'seq'), may hold values from -0.15 to 0.15
- lengths: int32 [16, 4], P('fsdp', 'seq'), may hold values from 112 to 128
- rewards: float32 [16, 4], P('fsdp', 'seq'), may hold values from -5 to 5
- prompt_ids: int32 [16, 4], P('fsdp', 'seq'), may hold values from 0 to 3, as said below
- placement: int32 [16, 4], P('fsdp', 'seq'), may hold values from 0 to 15, as said below
Outputs:
- grad_context: bfloat16 [16, 512, 2560], P('fsdp', 'seq')
- grad_weight: float32 [2560, 2560], P('fsdp')
- loss: float32 [], replicated
Inputs may be any that keep to these rules, and one draw needn't show every extreme that they name: `prompt_ids`: every prompt id names exactly 16 rows. Sampler row (a, s) goes to learner row (placement[a, s], s) and keeps a mod 2; the 2 rows of one device go to 2 different fsdp indices; every learner row receives exactly one row; in every column one of the 2 rows of each device goes 8 / 2 fsdp indices onward and another goes 1 index onward, counted round.
All inputs are finite; a program needn't handle non-finite values.
Results may differ from a plain program's by a relative error of at most 0.014.
Values may be sent and summed in bfloat16 or wider, within the bound.
A program may use at most 128 MiB of HBM per device.

v0:
```python
import math
import jax
import jax.numpy as jnp
from jax import lax
from jax.sharding import PartitionSpec as P

DW = 2560
AW = 2560
GS = 16


def body(
    context,
    residual,
    target_rows,
    log_norm,
    norm_gain,
    out_proj,
    old_logprob,
    lengths,
    rewards,
    prompt_ids,
    placement,
):
    nrows = context.shape[0]
    lmax = context.shape[1]
    fsdp_ways = lax.axis_size("fsdp")
    seq_ways = lax.axis_size("seq")
    prompts = nrows * fsdp_ways * seq_ways // GS
    all_tokens = nrows * lmax * fsdp_ways * seq_ways
    reward_flat = rewards.reshape(-1)
    prompt_flat = prompt_ids.reshape(-1)
    length_flat = lengths.reshape(-1)
    dest_flat = placement.reshape(-1)
    prompt_range = jnp.arange(prompts, dtype=jnp.int32)
    local_hot = (prompt_flat[:, None] == prompt_range[None, :]).astype(jnp.float32)
    group_sum, group_sq, count = lax.psum(
        (
            jnp.sum(local_hot * reward_flat[:, None], axis=0),
            jnp.sum(local_hot * (reward_flat * reward_flat)[:, None], axis=0),
            jnp.sum(length_flat.astype(jnp.float32)),
        ),
        ("fsdp", "seq"),
    )
    group_mean = group_sum / GS
    group_var = group_sq / GS - group_mean * group_mean
    row_mean = jnp.sum(local_hot * group_mean[None, :], axis=1)
    row_var = jnp.sum(local_hot * group_var[None, :], axis=1)
    advantage = (reward_flat - row_mean) / jnp.sqrt(row_var + 0.25)
    slots = jnp.arange(nrows, dtype=jnp.int32)
    every_old, every_adv, every_len, every_dest = (
        lax.all_gather(old_logprob, "fsdp", axis=0, tiled=True),
        lax.all_gather(advantage, "fsdp", axis=0, tiled=True),
        lax.all_gather(length_flat, "fsdp", axis=0, tiled=True),
        lax.all_gather(dest_flat, "fsdp", axis=0, tiled=True),
    )
    wanted = lax.axis_index("fsdp") * nrows + slots
    chosen = every_dest[None, :] == wanted[:, None]
    learn_old = jnp.sum(jnp.where(chosen[:, :, None], every_old[None, :, :], 0.0), axis=1)
    learn_adv = jnp.sum(jnp.where(chosen, every_adv[None, :], 0.0), axis=1)
    learn_len = jnp.sum(jnp.where(chosen, every_len[None, :], 0), axis=1)
    offsets = jnp.arange(lmax, dtype=jnp.int32)
    valid = (offsets[None, :] < learn_len[:, None]).astype(jnp.float32).reshape(-1)
    token_adv = jnp.broadcast_to(learn_adv[:, None], (nrows, lmax)).reshape(-1)
    tokens = nrows * lmax
    context_flat = context.reshape(tokens, AW)
    whole = lax.all_gather(out_proj, "fsdp", axis=0, tiled=True)
    hidden = residual.reshape(tokens, DW).astype(jnp.float32) + jnp.dot(
        context_flat, whole, preferred_element_type=jnp.float32
    )
    rinv = lax.rsqrt(jnp.mean(hidden * hidden, axis=1) + 1e-06)
    vecs = norm_gain[None, :] * target_rows.reshape(tokens, DW).astype(jnp.float32)
    hv_sum = jnp.sum(hidden * vecs, axis=1)
    score = hv_sum * rinv
    ratio = jnp.exp(score - log_norm.reshape(-1) - learn_old.reshape(-1))
    plain = ratio * token_adv
    clipped = jnp.clip(ratio, 0.8, 1.2) * token_adv
    objective = jnp.minimum(plain, clipped)
    loss_local = jnp.sum(valid * -objective)
    dscore = -valid * jnp.where(plain <= clipped, plain, 0.0) / count
    dhid = (dscore * rinv)[:, None] * (vecs - hidden * (rinv * rinv * hv_sum / DW)[:, None])
    grad_hidden = (dhid * (32.0 * all_tokens * math.sqrt(DW))).astype(jnp.bfloat16)
    grad_context = lax.dot_general(
        grad_hidden, whole, (((1,), (1,)), ((), ())), preferred_element_type=jnp.float32
    ).astype(jnp.bfloat16)
    piece = lax.psum_scatter(
        lax.dot_general(
            context_flat, grad_hidden, (((0,), (0,)), ((), ())), preferred_element_type=jnp.float32
        ).astype(jnp.bfloat16),
        "fsdp",
        scatter_dimension=0,
        tiled=True,
    )
    grad_weight = lax.psum(piece, "seq").astype(jnp.float32) * (1.0 / math.sqrt(all_tokens))
    loss = lax.psum(loss_local, ("fsdp", "seq")) / count
    return (grad_context.reshape(nrows, lmax, AW), grad_weight, loss)


def solution(mesh):
    return jax.shard_map(
        body,
        mesh=mesh,
        in_specs=(
            P("fsdp", "seq", None),
            P("fsdp", "seq", None),
            P("fsdp", "seq", None),
            P("fsdp", "seq"),
            P(),
            P("fsdp", None),
            P("fsdp", "seq"),
            P("fsdp", "seq"),
            P("fsdp", "seq"),
            P("fsdp", "seq"),
            P("fsdp", "seq"),
        ),
        out_specs=(P("fsdp", "seq", None), P("fsdp", None), P()),
        check_vma=False,
    )
```

profile of v0, /device:TPU:0, one launch (start us, length us, event | category | flops | bytes accessed | tf_op | source)
XLA Modules:
  0.0 559.2 jit_solution(6872598172934750625)
XLA Ops:
  7.2 0.7 all-gather.5.cloned.1.call-update
  7.9 0.0 reduce-scatter.4.cloned.1.call-start
  8.0 0.7 multiply_bitcast_fusion
  8.6 0.8 select_reduce_fusion.6
  9.4 46.3 %all-reduce.5 = (f32[4]{0:T(128)S(1)}, f32[4]{0:T(128)S(1)}) all-reduce(f32[4]{0:T(128)S(1)} %get-tuple-element.16, f32[4]{0:T(128)S(1)} %get-tuple-element.17), channel_id=1, replica_groups=mesh['fsdp'=8,'seq'=4] {'fsdp','seq'}, use_global_device_ids=true, to_apply=%region_5.0 | all-reduce | flops 8 | bytes 64 | tf_op jit(solution)/shard_map/psum | solution.py:37
  55.7 1.2 dynamic-slice
  57.6 0.9 select_reduce_fusion.5
  58.5 0.8 bitcast_dynamic-update-slice_fusion.1
  59.2 0.7 multiply_dynamic-update-slice_fusion
  60.0 0.7 bitcast_dynamic-update-slice_fusion
  60.7 20.1 %all-reduce.2 = f32[16]{0:T(128)S(1)} all-reduce(f32[16]{0:T(128)S(1)} %multiply_dynamic-update-slice_fusion), channel_id=1, replica_groups=mesh['fsdp'=8,'seq'=4] {'fsdp'}, use_global_device_ids=true, to_apply=%add.2 | all-reduce | flops 16 | bytes 128
  80.9 12.8 %all-reduce.3 = (s32[16]{0:T(128)S(1)}, s32[16]{0:T(128)S(1)}) all-reduce(s32[16]{0:T(128)S(1)} %bitcast_dynamic-update-slice_fusion.1, s32[16]{0:T(128)S(1)} %bitcast_dynamic-update-slice_fusion), channel_id=2, replica_groups=mesh['fsdp'=8,'seq'=4] {'fsdp'}, use_global_device_ids=true, to_apply=%add | all-reduce | flops 32 | bytes 256
  93.7 18.2 %all-gather.2 = f32[8,2,128]{2,1,0:T(2,128)S(1)} all-gather(f32[1,2,128]{2,1,0:T(2,128)} %bitcast.68), channel_id=1, replica_groups=mesh['fsdp'=8,'seq'=4] {'fsdp'}, dimensions={0}, use_global_device_ids=true | all-gather | bytes 9216 | tf_op jit(solution)/shard_map/all_gather | solution.py:52
  111.9 1.3 convert_reduce_fusion
  113.1 0.2 select_reduce_fusion.2
  113.3 0.1 select_reduce_fusion.7
  113.4 0.1 select_reduce_fusion
  113.5 83.5 %all-gather.5.cloned.1.call-done = bf16[2560,2560]{1,0:T(8,128)(2,1)} async-done(((bf16[320,2560]{1,0:T(8,128)(2,1)}), bf16[2560,2560]{1,0:T(8,128)(2,1)}) %all-gather.5.cloned.1.call-update) | async-done | bytes 13107216 | tf_op jit(solution)/shard_map/all_gather | solution.py:67
  197.0 10.4 %multiply_reduce_fusion = (f32[256]{0:T(256)S(1)}, f32[256]{0:T(256)S(1)}, f32[256,2560]{1,0:T(8,128)}) fusion(bf16[2,128,2560]{2,1,0:T(8,128)(2,1)} %param.13, f32[2560]{0:T(1024)} %param.15, bf16[256,2560]{1,0:T(8,128)(2,1)S(1)} %bitcast.62, bf16[2560,2560]{1,0:T(8,128)(2,1)} %all-gather.5.cloned.1.call-done, bf16[256,2560]{1,0:T(8,128)(2,1)} %bitcast.69), kind=kOutput, calls=%fused_computation.12 | convolution fusion | flops 3360685568 | bytes 19673088 | tf_op jit(solution)/shard_map/dot_general | solution.py:68
  207.4 0.7 select_reduce_fusion.1
  208.1 38.7 %all-reduce.4 = (f32[]{:T(128)}, f32[]{:T(128)}) all-reduce(f32[]{:T(128)} %convert_reduce_fusion, f32[]{:T(128)} %select_reduce_fusion.1), channel_id=1, replica_groups=mesh['fsdp'=8,'seq'=4] {'fsdp','seq'}, use_global_device_ids=true, to_apply=%region_12.13 | all-reduce | flops 2 | bytes 16 | tf_op jit(solution)/shard_map/psum | solution.py:37
  246.7 0.7 divide_multiply_fusion
  247.5 2.7 fusion.6
  250.2 6.8 %fusion = bf16[2560,2560]{0,1:T(8,128)(2,1)} fusion(bf16[256,2560]{1,0:T(8,128)(2,1)S(1)} %fusion.6, bf16[256,2560]{1,0:T(8,128)(2,1)S(1)} %bitcast.63), kind=kOutput, calls=%fused_computation.1 | convolution fusion | flops 3361996800 | bytes 15728640 | tf_op jit(solution)/shard_map/dot_general | solution.py:87
  257.0 17.6 %copy.17 = bf16[2560,2560]{1,0:T(8,128)(2,1)} copy(bf16[2560,2560]{0,1:T(8,128)(2,1)} %fusion) | data formatting | bytes 26214400
  274.6 0.0 all-reduce.8.cloned.1.call-start
  276.0 214.2 %reduce-scatter.4.cloned.1.call-done = bf16[320,2560]{1,0:T(8,128)(2,1)} async-done(((bf16[2560,2560]{1,0:T(8,128)(2,1)}), bf16[320,2560]{1,0:T(8,128)(2,1)}) %reduce-scatter.4.cloned.1.call-update) | async-done | bytes 1638416
  490.2 3.8 copy.18
  494.0 9.4 %convolution_convert_fusion.1 = bf16[256,2560]{1,0:T(8,128)(2,1)} fusion(bf16[256,2560]{1,0:T(8,128)(2,1)S(1)} %fusion.6, bf16[2560,2560]{1,0:T(8,128)(2,1)} %all-gather.5.cloned.1.call-done), kind=kOutput, calls=%fused_computation.4 | convolution fusion | flops 3356098560 | bytes 15728640 | tf_op jit(solution)/shard_map/dot_general | solution.py:83
  503.4 39.1 %all-reduce.8.cloned.1.call-done = bf16[320,2560]{0,1:T(8,128)(2,1)} async-done(((bf16[320,2560]{0,1:T(8,128)(2,1)}), bf16[320,2560]{0,1:T(8,128)(2,1)}) %all-reduce.8.cloned.1.call-update) | async-done | bytes 1638416 | tf_op jit(solution)/shard_map/psum | solution.py:94
  542.6 3.8 convert_multiply_fusion
  546.3 5.2 copy.16
  (14 shorter events, 0.1 us)
Async XLA Ops:
  7.2 189.9 %copy-start = (bf16[2,128,2560]{2,1,0:T(8,128)(2,1)S(1)}, bf16[2,128,2560]{2,1,0:T(8,128)(2,1)}, u32[]{:S(2)}) copy-start(bf16[2,128,2560]{2,1,0:T(8,128)(2,1)} %param.11) | copy-start | bytes 3932164
  7.2 189.9 %all-gather.5.cloned.1.call-start = ((), (), s32[]{:S(2)}) async-start(), calls=%async_computation.1 | async-start | bytes 14745600 | tf_op jit(solution)/shard_map/all_gather | solution.py:67
  7.9 482.3 %reduce-scatter.4.cloned.1.call-start = ((), (), s32[]{:S(2)}) async-start(), calls=%async_computation.3 | async-start | bytes 14745600
  197.0 10.4 %copy-start.2 = (f32[2,128]{1,0:T(2,128)S(1)}, f32[2,128]{1,0:T(2,128)}, u32[]{:S(2)}) copy-start(f32[2,128]{1,0:T(2,128)} %param.14) | copy-start | bytes 3076
  197.0 50.4 %copy-start.1 = (f32[2560]{0:T(1024)S(1)}, f32[2560]{0:T(1024)}, u32[]{:S(2)}) copy-start(f32[2560]{0:T(1024)} %param.15) | copy-start | bytes 30724
  274.6 267.9 %all-reduce.8.cloned.1.call-start = ((), (), s32[]{:S(2)}) async-start(), calls=%async_computation.2 | async-start | bytes 3932160 | tf_op jit(solution)/shard_map/psum | solution.py:94
Sparse Core Ops, SparseCore 0:
  10.2 186.7 all-gather.4
  274.7 215.4 reduce-scatter.3
  494.2 48.3 all-reduce.7
where the time goes:
time: 560 us; the launch traced here: 559 us
  waiting for transfers between devices  338 us (60%)
  blocking collectives  136 us (24%)
  local copies, waits for them, and re-layouts  29.4 us (5%)
  matrix products  26.5 us (5%)
  between operations  16.9 us (3%)
  other arithmetic  12.6 us (2%)
    unnamed x4, waiting for transfers between devices  215 us
    psum x2, blocking collectives, body(): lax.psum((jnp.sum(local_hot * reward_flat[:, None], axis=0), jnp.sum(loca...  85 us
    all_gather x1, waiting for transfers between devices, body(): whole = lax.all_gather(out_proj, 'fsdp', axis=0, tiled=True)  83.5 us
    psum x1, waiting for transfers between devices, body(): lax.psum(piece, 'seq').astype(jnp.float32) * (1.0 / math.sqrt(all_tokens))  39.1 us
    unnamed x2, blocking collectives  33 us
    unnamed x15, local copies, waits for them, and re-layouts  29.4 us
    all_gather x1, blocking collectives, body(): lax.all_gather(old_logprob, 'fsdp', axis=0, tiled=True)  18.2 us
  transfers between devices with their start and end apart: 3, of which 3 were waited for; matrix products, arithmetic and copies ran while one was open for 3% of the time, Pallas kernels for 0%

commit v1 on v0

--- a/solution.py
+++ b/solution.py
@@ -35,12 +35,15 @@
     prompt_range = jnp.arange(prompts, dtype=jnp.int32)
     local_hot = (prompt_flat[:, None] == prompt_range[None, :]).astype(jnp.float32)
     group_sum, group_sq, count = lax.psum(
-        (
-            jnp.sum(local_hot * reward_flat[:, None], axis=0),
-            jnp.sum(local_hot * (reward_flat * reward_flat)[:, None], axis=0),
-            jnp.sum(length_flat.astype(jnp.float32)),
+        lax.psum(
+            (
+                jnp.sum(local_hot * reward_flat[:, None], axis=0),
+                jnp.sum(local_hot * (reward_flat * reward_flat)[:, None], axis=0),
+                jnp.sum(length_flat.astype(jnp.float32)),
+            ),
+            "seq",
         ),
-        ("fsdp", "seq"),
+        "fsdp",
     )
     group_mean = group_sum / GS
     group_var = group_sq / GS - group_mean * group_mean

time: 560 us -> 515 us (0.920)
  waiting for transfers between devices: 338 us -> 308 us
  blocking collectives: 136 us -> 123 us
    psum x0 -> x3, blocking collectives: none -> 82.9 us  [the longest x1 42.1 us: body(): loss = lax.psum(loss_local, ('fsdp', 'seq')) / count]
    psum x2 -> x1, blocking collectives: 85 us -> 9.01 us  [body(): lax.psum((jnp.sum(local_hot * reward_flat[:, None], axis=0), jnp.sum(loca...]
    unnamed x4, waiting for transfers between devices: 215 us -> 170 us
    unnamed x2 -> x1, blocking collectives: 33 us -> 8.75 us
    all_gather x1, waiting for transfers between devices: 83.5 us -> 99 us  [body(): whole = lax.all_gather(out_proj, 'fsdp', axis=0, tiled=True)]
    unnamed x15 -> x17, local copies, waits for them, and re-layouts: 29.4 us -> 29.4 us
where the time goes in v1:
time: 515 us; the launch traced here: 514 us
  waiting for transfers between devices  308 us (60%)
  blocking collectives  123 us (24%)
  local copies, waits for them, and re-layouts  29.4 us (6%)
  matrix products  25.5 us (5%)
  between operations  16.9 us (3%)
  other arithmetic  10.5 us (2%)
    unnamed x4, waiting for transfers between devices  170 us
    all_gather x1, waiting for transfers between devices, body(): whole = lax.all_gather(out_proj, 'fsdp', axis=0, tiled=True)  99 us
    psum x1, blocking collectives, body(): loss = lax.psum(loss_local, ('fsdp', 'seq')) / count  42.1 us
    psum x2, blocking collectives, body(): lax.psum(lax.psum((jnp.sum(local_hot * reward_flat[:, None], axis=0), jnp...  40.8 us
    psum x1, waiting for transfers between devices, body(): lax.psum(piece, 'seq').astype(jnp.float32) * (1.0 / math.sqrt(all_tokens))  39.1 us
    unnamed x17, local copies, waits for them, and re-layouts  29.4 us
    all_gather x1, blocking collectives, body(): lax.all_gather(old_logprob, 'fsdp', axis=0, tiled=True)  22.8 us
  transfers between devices with their start and end apart: 3, of which 3 were waited for; matrix products, arithmetic and copies ran while one was open for 3% of the time, Pallas kernels for 0%

profile of v1, /device:TPU:0, one launch (start us, length us, event | category | flops | bytes accessed | tf_op | source)
XLA Modules:
  0.0 514.3 jit_solution(12142992902419565538)
XLA Ops:
  7.2 0.7 all-gather.5.cloned.1.call-update
  8.0 1.3 convert_reduce_fusion
  9.2 0.7 multiply_bitcast_fusion
  9.9 0.8 select_reduce_fusion.6
  10.6 9.0 %all-reduce.6 = (f32[]{:T(128)}, f32[4]{0:T(128)S(1)}, f32[4]{0:T(128)S(1)}) all-reduce(f32[]{:T(128)} %convert_reduce_fusion, f32[4]{0:T(128)S(1)} %get-tuple-element.16, f32[4]{0:T(128)S(1)} %get-tuple-element.17), channel_id=1, replica_groups=mesh['fsdp'=8,'seq'=4] {'seq'}, use_global_device_ids=true, to_apply=%region_14.15 | all-reduce | flops 9 | bytes 72 | tf_op jit(solution)/shard_map/psum | solution.py:38
  19.6 22.4 %all-reduce.5 = (f32[4]{0:T(128)S(1)}, f32[4]{0:T(128)S(1)}) all-reduce(f32[4]{0:T(128)S(1)} %get-tuple-element.25, f32[4]{0:T(128)S(1)} %get-tuple-element.26), channel_id=1, replica_groups=mesh['fsdp'=8,'seq'=4] {'fsdp'}, use_global_device_ids=true, to_apply=%region_6.0 | all-reduce | flops 8 | bytes 64 | tf_op jit(solution)/shard_map/psum | solution.py:37
  42.1 1.2 dynamic-slice
  44.0 0.9 select_reduce_fusion.5
  44.8 0.8 bitcast_dynamic-update-slice_fusion
  45.6 0.7 bitcast_dynamic-update-slice_fusion.1
  46.3 0.7 multiply_dynamic-update-slice_fusion
  47.1 18.4 %all-reduce.4 = (f32[]{:T(128)}, f32[16]{0:T(128)S(1)}) all-reduce(f32[]{:T(128)} %get-tuple-element.24, f32[16]{0:T(128)S(1)} %multiply_dynamic-update-slice_fusion), channel_id=1, replica_groups=mesh['fsdp'=8,'seq'=4] {'fsdp'}, use_global_device_ids=true, to_apply=%region_15.16 | all-reduce | flops 17 | bytes 136 | tf_op jit(solution)/shard_map/psum | solution.py:37
  65.5 8.8 %all-reduce.3 = (s32[16]{0:T(128)S(1)}, s32[16]{0:T(128)S(1)}) all-reduce(s32[16]{0:T(128)S(1)} %bitcast_dynamic-update-slice_fusion.1, s32[16]{0:T(128)S(1)} %bitcast_dynamic-update-slice_fusion), channel_id=2, replica_groups=mesh['fsdp'=8,'seq'=4] {'fsdp'}, use_global_device_ids=true, to_apply=%add | all-reduce | flops 32 | bytes 256
  74.2 22.8 %all-gather.2 = f32[8,2,128]{2,1,0:T(2,128)S(1)} all-gather(f32[1,2,128]{2,1,0:T(2,128)} %bitcast.68), channel_id=1, replica_groups=mesh['fsdp'=8,'seq'=4] {'fsdp'}, dimensions={0}, use_global_device_ids=true | all-gather | bytes 9216 | tf_op jit(solution)/shard_map/all_gather | solution.py:55
  97.0 0.2 select_reduce_fusion.2
  97.2 0.1 select_reduce_fusion.7
  97.3 0.1 select_reduce_fusion
  97.4 99.0 %all-gather.5.cloned.1.call-done = bf16[2560,2560]{1,0:T(8,128)(2,1)} async-done(((bf16[320,2560]{1,0:T(8,128)(2,1)}), bf16[2560,2560]{1,0:T(8,128)(2,1)}) %all-gather.5.cloned.1.call-update) | async-done | bytes 13107216 | tf_op jit(solution)/shard_map/all_gather | solution.py:70
  196.4 9.3 %multiply_reduce_fusion = (f32[256]{0:T(256)S(1)}, f32[256]{0:T(256)S(1)}, f32[256,2560]{1,0:T(8,128)S(1)}) fusion(bf16[2,128,2560]{2,1,0:T(8,128)(2,1)} %param.13, f32[2560]{0:T(1024)} %param.15, bf16[256,2560]{1,0:T(8,128)(2,1)S(1)} %bitcast.62, bf16[2560,2560]{1,0:T(8,128)(2,1)} %all-gather.5.cloned.1.call-done, bf16[256,2560]{1,0:T(8,128)(2,1)} %bitcast.69), kind=kOutput, calls=%fused_computation.12 | convolution fusion | flops 3360685568 | bytes 19673088 | tf_op jit(solution)/shard_map/dot_general | solution.py:71
  205.8 0.7 divide_multiply_fusion
  206.5 0.7 fusion.6
  207.2 6.8 %fusion = bf16[2560,2560]{0,1:T(8,128)(2,1)} fusion(bf16[256,2560]{1,0:T(8,128)(2,1)S(1)} %fusion.6, bf16[256,2560]{1,0:T(8,128)(2,1)S(1)} %bitcast.63), kind=kOutput, calls=%fused_computation.1 | convolution fusion | flops 3361996800 | bytes 15728640 | tf_op jit(solution)/shard_map/dot_general | solution.py:90
  214.0 17.6 %copy.17 = bf16[2560,2560]{1,0:T(8,128)(2,1)} copy(bf16[2560,2560]{0,1:T(8,128)(2,1)} %fusion) | data formatting | bytes 26214400
  231.7 0.0 all-reduce.9.cloned.1.call-start
  231.7 0.7 select_reduce_fusion.1
  232.4 42.1 %psum.63 = f32[]{:T(128)} all-reduce(f32[]{:T(128)} %select_reduce_fusion.1), channel_id=1, replica_groups=mesh['fsdp'=8,'seq'=4] {'fsdp','seq'}, use_global_device_ids=true, to_apply=%region_19.20 | all-reduce | flops 1 | bytes 8 | tf_op jit(solution)/shard_map/psum | solution.py:98
  275.8 169.4 %reduce-scatter.4.cloned.1.call-done = bf16[320,2560]{1,0:T(8,128)(2,1)} async-done(((bf16[2560,2560]{1,0:T(8,128)(2,1)}), bf16[320,2560]{1,0:T(8,128)(2,1)}) %reduce-scatter.4.cloned.1.call-update) | async-done | bytes 1638416
  445.3 3.8 copy.18
  449.1 9.4 %convolution_convert_fusion.1 = bf16[256,2560]{1,0:T(8,128)(2,1)} fusion(bf16[256,2560]{1,0:T(8,128)(2,1)S(1)} %fusion.6, bf16[2560,2560]{1,0:T(8,128)(2,1)} %all-gather.5.cloned.1.call-done), kind=kOutput, calls=%fused_computation.4 | convolution fusion | flops 3356098560 | bytes 15728640 | tf_op jit(solution)/shard_map/dot_general | solution.py:86
  458.5 39.1 %all-reduce.9.cloned.1.call-done = bf16[320,2560]{0,1:T(8,128)(2,1)} async-done(((bf16[320,2560]{0,1:T(8,128)(2,1)}), bf16[320,2560]{0,1:T(8,128)(2,1)}) %all-reduce.9.cloned.1.call-update) | async-done | bytes 1638416 | tf_op jit(solution)/shard_map/psum | solution.py:97
  497.6 3.8 convert_multiply_fusion
  501.4 5.2 %copy.16 = f32[320,2560]{1,0:T(8,128)} copy(f32[320,2560]{0,1:T(8,128)} %convert_multiply_fusion) | data formatting | bytes 6553600
  (17 shorter events, 0.1 us)
Async XLA Ops:
  7.2 189.3 %copy-start = (bf16[2,128,2560]{2,1,0:T(8,128)(2,1)S(1)}, bf16[2,128,2560]{2,1,0:T(8,128)(2,1)}, u32[]{:S(2)}) copy-start(bf16[2,128,2560]{2,1,0:T(8,128)(2,1)} %param.11) | copy-start | bytes 3932164
  7.2 189.3 %all-gather.5.cloned.1.call-start = ((), (), s32[]{:S(2)}) async-start(), calls=%async_computation.1 | async-start | bytes 14745600 | tf_op jit(solution)/shard_map/all_gather | solution.py:70
  7.9 437.4 %reduce-scatter.4.cloned.1.call-start = ((), (), s32[]{:S(2)}) async-start(), calls=%async_computation.3 | async-start | bytes 14745600
  196.4 9.4 %copy-start.3 = (f32[2,128]{1,0:T(2,128)S(1)}, f32[2,128]{1,0:T(2,128)}, u32[]{:S(2)}) copy-start(f32[2,128]{1,0:T(2,128)} %param.14) | copy-start | bytes 3076
  196.4 10.1 %copy-start.1 = (bf16[2,128,2560]{2,1,0:T(8,128)(2,1)S(1)}, bf16[2,128,2560]{2,1,0:T(8,128)(2,1)}, u32[]{:S(2)}) copy-start(bf16[2,128,2560]{2,1,0:T(8,128)(2,1)} %param.13) | copy-start | bytes 3932164
  196.4 10.1 %copy-start.2 = (f32[2560]{0:T(1024)S(1)}, f32[2560]{0:T(1024)}, u32[]{:S(2)}) copy-start(f32[2560]{0:T(1024)} %param.15) | copy-start | bytes 30724
  231.7 266.0 %all-reduce.9.cloned.1.call-start = ((), (), s32[]{:S(2)}) async-start(), calls=%async_computation.2 | async-start | bytes 3932160 | tf_op jit(solution)/shard_map/psum | solution.py:97
Sparse Core Ops, SparseCore 0:
  10.2 186.1 all-gather.4
  231.8 213.4 reduce-scatter.3
  449.3 48.3 all-reduce.8
